TPU v7x, 512 devices: a whole 4x8x8 slice. The times are simulated.
512 devices in a mesh: expert: 8 (over z_lo, x), fsdp: 64 (over z_hi, y, core).
Axes of the slice: x: 4, y: 8, z: 8 (z_hi: 4, z_lo: 2; z = z_hi * 2 + z_lo), core: 2. Of those that a mesh axis runs over, the one named last changes fastest.
Arguments:
- dense_rows: bfloat16 [128, 14336], P('fsdp', 'expert'), may hold values from -6 to 6
- noise: bfloat16 [8, 128, 14336], P('expert', 'fsdp'), may hold values from -6 to 6
- features: bfloat16 [8, 8192, 128], P('expert', 'fsdp'), may hold values from -16 to 16
- out_grads: bfloat16 [8, 8192, 14336], P('expert', 'fsdp'), may hold values from -1 to 1
Outputs:
- master: float32 [8, 128, 14336], P('expert', 'fsdp')
- first_moment: float32 [8, 128, 14336], P('expert', 'fsdp')
- second_moment: float32 [8, 128, 14336], P('expert', 'fsdp')
- expert_copy: bfloat16 [8, 128, 14336], P('expert')
All inputs are finite; a program needn't handle non-finite values.
Results may differ from a plain program's by a relative error of at most 0.004.
Values may be sent and summed in bfloat16 or wider, within the bound.
No kernel may reach another device: no remote copies, remote signals or barrier semaphores. Data moves between devices by JAX's collectives and lax.ppermute only.
A program may use at most 64 MiB of HBM per device.

v0:
```python
import jax
import jax.numpy as jnp
from jax import lax
from jax.sharding import PartitionSpec as P

noise_scale = 0.1
first_decay = 0.9
second_decay = 0.95
learn_rate = 0.2
weight_decay = 0.5
epsilon_adam = 1.0


def adamw(initial, gradient):
    first_moment = (1.0 - first_decay) * gradient
    second_moment = (1.0 - second_decay) * gradient * gradient
    update = (
        first_moment
        / (1.0 - first_decay)
        / (jnp.sqrt(second_moment / (1.0 - second_decay)) + epsilon_adam)
    )
    master = initial - learn_rate * (update + weight_decay * initial)
    return (master, first_moment, second_moment)


def body(dense_rows, noise, features, out_grads):
    dense_full = lax.all_gather(dense_rows, "expert", axis=1, tiled=True)
    initial = dense_full.astype(jnp.float32)[None] + noise_scale * noise.astype(jnp.float32)
    inputs_local = features[0]
    grads_local = out_grads[0]
    product = lax.dot_general(
        inputs_local, grads_local, (((0,), (0,)), ((), ())), preferred_element_type=jnp.float32
    )
    gradient = lax.psum_scatter(
        lax.optimization_barrier(product.astype(jnp.bfloat16)).astype(jnp.float32),
        "fsdp",
        scatter_dimension=0,
        tiled=True,
    )
    master, first_moment, second_moment = adamw(initial, gradient[None])
    expert_copy = lax.all_gather(master.astype(jnp.bfloat16), "fsdp", axis=1, tiled=True)
    return (master, first_moment, second_moment, expert_copy)


def solution(mesh):
    return jax.shard_map(
        body,
        mesh=mesh,
        in_specs=(
            P("fsdp", "expert"),
            P("expert", "fsdp", None),
            P("expert", "fsdp", None),
            P("expert", "fsdp", None),
        ),
        out_specs=(
            P("expert", "fsdp", None),
            P("expert", "fsdp", None),
            P("expert", "fsdp", None),
            P("expert", None, None),
        ),
        check_vma=False,
    )
```

profile of v0, /device:TPU:1, one launch (start us, length us, event | category | flops | bytes accessed | tf_op | source)
XLA Modules:
  0.0 503.9 jit_solution(10311162020342887844)
XLA Ops:
  7.2 0.0 copy-start
  7.2 0.0 all-gather.2.cloned.1.call-start
  7.2 0.7 copy-done
  7.9 5.0 convolution_convert_fusion
  12.9 0.0 copy-start.2
  12.9 0.0 copy-start.1
  13.0 339.0 %all-reduce.2 = f32[128,14336]{1,0:T(8,128)} all-reduce(bf16[128,14336]{1,0:T(8,128)(2,1)} %convolution_convert_fusion), channel_id=2, replica_groups=mesh['expert'=8,'fsdp'=64] {'fsdp'}, use_global_device_ids=true, to_apply=%region_0.0.clone | all-reduce | flops 1835008 | bytes 11010048
  352.0 0.0 copy-done.2
  352.0 29.0 %all_gather.6 = bf16[2,14336]{1,0:T(2,128)(2,1)S(1)} all-gather(bf16[2,1792]{1,0:T(2,128)(2,1)S(1)} %copy-done.2), channel_id=1, replica_groups=mesh['expert'=8,'fsdp'=64] {'expert'}, dimensions={1}, use_global_device_ids=true | all-gather | bytes 64512 | tf_op jit(solution)/shard_map/all_gather | solution.py:27
  381.0 1.3 dynamic-slice
  382.9 0.0 copy-done.1
  382.9 2.0 fusion.5
  384.9 0.7 copy.8
  385.7 0.0 all-gather.2.cloned.1.call-update
  385.7 1.8 fusion.3
  387.5 102.6 %all-gather.2.cloned.1.call-done = bf16[1,128,14336]{2,0,1:T(2,128)(2,1)} async-done(((bf16[1,2,14336]{2,0,1:T(2,128)(2,1)}), bf16[1,128,14336]{2,0,1:T(2,128)(2,1)}) %all-gather.2.cloned.1.call-update) | async-done | bytes 3670032 | tf_op jit(solution)/shard_map/all_gather | solution.py:41
  490.1 7.0 %copy.9 = bf16[1,128,14336]{2,1,0:T(8,128)(2,1)} copy(bf16[1,128,14336]{2,0,1:T(2,128)(2,1)} %all-gather.2.cloned.1.call-done) | data formatting | bytes 7340032
Async XLA Ops:
  7.2 0.8 copy-start
  7.2 482.9 %all-gather.2.cloned.1.call-start = ((), (), s32[]{:S(2)}) async-start(), calls=%async_computation | async-start | bytes 7454720 | tf_op jit(solution)/shard_map/all_gather | solution.py:41
  12.9 339.0 %copy-start.2 = (bf16[2,1792]{1,0:T(2,128)(2,1)S(1)}, bf16[2,1792]{1,0:T(2,128)(2,1)}, u32[]{:S(2)}) copy-start(bf16[2,1792]{1,0:T(2,128)(2,1)} %param.4) | copy-start | bytes 21508
  12.9 369.9 %copy-start.1 = (bf16[1,2,14336]{2,1,0:T(2,128)(2,1)S(1)}, bf16[1,2,14336]{2,1,0:T(2,128)(2,1)}, u32[]{:S(2)}) copy-start(bf16[1,2,14336]{2,1,0:T(2,128)(2,1)} %param.5) | copy-start | bytes 172036
Sparse Core Ops, SparseCore 0:
  385.8 104.2 all-gather.1
where the time goes:
time: 504 us
  blocking collectives  368 us (73%)
  waiting for transfers between devices  103 us (20%)
  between operations  14.7 us (3%)
  local copies, waits for them, and re-layouts  9.7 us (2%)
    unnamed x1, blocking collectives  339 us
    all_gather x1, waiting for transfers between devices, body(): lax.all_gather(master.astype(jnp.bfloat16), 'fsdp', axis=1, tiled=True)  103 us
    all_gather x1, blocking collectives, body(): dense_full = lax.all_gather(dense_rows, 'expert', axis=1, tiled=True)  29 us
  transfers between devices with their start and end apart: 1, of which 1 were waited for; matrix products, arithmetic and copies ran while one was open for 0% of the time, Pallas kernels for 0%

commit v1 on v0

--- a/solution.py
+++ b/solution.py
@@ -24,7 +24,9 @@
 
 
 def body(dense_rows, noise, features, out_grads):
-    dense_full = lax.all_gather(dense_rows, "expert", axis=1, tiled=True)
+    dense_full = jnp.concatenate(
+        lax.all_to_all(jnp.stack([dense_rows] * lax.axis_size("expert")), "expert", 0, 0), axis=1
+    )
     initial = dense_full.astype(jnp.float32)[None] + noise_scale * noise.astype(jnp.float32)
     inputs_local = features[0]
     grads_local = out_grads[0]

time: 504 us -> 482 us (0.956)
  blocking collectives: 368 us -> 338 us
  starting transfers between devices: 0.04 us -> 6.69 us
    all_gather x1 -> x0, blocking collectives: 29 us -> none  [body(): dense_full = lax.all_gather(dense_rows, 'expert', axis=1, tiled=True)]
    all_to_all x0 -> x1, starting transfers between devices: none -> 6.66 us  [body(): lax.all_to_all(jnp.stack([dense_rows] * lax.axis_size('expert')), 'expert...]
  transfers between devices with their start and end apart: 1 -> 2, of which waited for: 1 -> 1; matrix products, arithmetic and copies ran while one was open for 0% -> 2% of each run, Pallas kernels for 0% -> 0%
where the time goes in v1:
time: 482 us; the launch traced here: 481 us
  blocking collectives  338 us (70%)
  waiting for transfers between devices  102 us (21%)
  between operations  14.7 us (3%)
  local copies, waits for them, and re-layouts  10.4 us (2%)
  starting transfers between devices  6.69 us (1%)
  matrix products  5.02 us (1%)
    unnamed x1, blocking collectives  338 us
    all_gather x1, waiting for transfers between devices, body(): lax.all_gather(master.astype(jnp.bfloat16), 'fsdp', axis=1, tiled=True)  102 us
  transfers between devices with their start and end apart: 2, of which 1 were waited for; matrix products, arithmetic and copies ran while one was open for 2% of the time, Pallas kernels for 0%

profile of v1, /device:TPU:1, one launch (start us, length us, event | category | flops | bytes accessed | tf_op | source)
XLA Modules:
  0.0 481.1 jit_solution(3516269588445589250)
XLA Ops:
  7.2 0.0 copy-start
  7.2 1.4 stack.2
  8.5 6.7 %all-to-all-start = ((bf16[8,2,1792]{2,1,0:T(2,128)(2,1)}), bf16[8,2,1792]{2,1,0:T(2,128)(2,1)S(1)}, u32[]{:S(2)}, u32[]{:S(2)}) async-start(bf16[8,2,1792]{2,1,0:T(2,128)(2,1)} %stack.2), calls=%async_computation | async-start | bytes 114688 | tf_op jit(solution)/shard_map/all_to_all | solution.py:28
  15.2 0.0 all-gather.2.cloned.1.call-start
  15.2 0.0 copy-done
  15.2 5.0 %convolution_convert_fusion = bf16[128,14336]{1,0:T(8,128)(2,1)} fusion(bf16[1,128,14336]{2,1,0:T(8,128)(2,1)} %param.7, bf16[1,128,128]{2,1,0:T(8,128)(2,1)S(1)} %copy-done), kind=kOutput, calls=%fused_computation | convolution fusion | flops 471597056 | bytes 7372800 | tf_op jit(solution)/shard_map/dot_general | solution.py:33
  20.3 0.0 copy-start.1
  20.3 337.9 %all-reduce.2 = f32[128,14336]{1,0:T(8,128)} all-reduce(bf16[128,14336]{1,0:T(8,128)(2,1)} %convolution_convert_fusion), channel_id=2, replica_groups=mesh['expert'=8,'fsdp'=64] {'fsdp'}, use_global_device_ids=true, to_apply=%region_0.0.clone | all-reduce | flops 1835008 | bytes 11010048
  358.2 1.3 dynamic-slice
  360.1 0.0 all-to-all-done
  360.2 0.0 copy-done.1
  360.2 2.0 fusion.5
  362.2 0.7 copy.8
  363.0 0.0 all-gather.2.cloned.1.call-update
  363.0 1.8 fusion.3
  364.8 102.4 %all-gather.2.cloned.1.call-done = bf16[1,128,14336]{2,0,1:T(2,128)(2,1)} async-done(((bf16[1,2,14336]{2,0,1:T(2,128)(2,1)}), bf16[1,128,14336]{2,0,1:T(2,128)(2,1)}) %all-gather.2.cloned.1.call-update) | async-done | bytes 3670032 | tf_op jit(solution)/shard_map/all_gather | solution.py:43
  467.2 7.0 %copy.9 = bf16[1,128,14336]{2,1,0:T(8,128)(2,1)} copy(bf16[1,128,14336]{2,0,1:T(2,128)(2,1)} %all-gather.2.cloned.1.call-done) | data formatting | bytes 7340032
  (1 shorter events, 0.0 us)
Async XLA Ops:
  7.2 8.1 %copy-start = (bf16[1,128,128]{2,1,0:T(8,128)(2,1)S(1)}, bf16[1,128,128]{2,1,0:T(8,128)(2,1)}, u32[]{:S(2)}) copy-start(bf16[1,128,128]{2,1,0:T(8,128)(2,1)} %param.6) | copy-start | bytes 98308
  8.5 351.6 %all-to-all-start = ((bf16[8,2,1792]{2,1,0:T(2,128)(2,1)}), bf16[8,2,1792]{2,1,0:T(2,128)(2,1)S(1)}, u32[]{:S(2)}, u32[]{:S(2)}) async-start(bf16[8,2,1792]{2,1,0:T(2,128)(2,1)} %stack.2), calls=%async_computation | async-start | bytes 114688 | tf_op jit(solution)/shard_map/all_to_all | solution.py:28
  15.2 452.0 %all-gather.2.cloned.1.call-start = ((), (), s32[]{:S(2)}) async-start(), calls=%async_computation.1 | async-start | bytes 7454720 | tf_op jit(solution)/shard_map/all_gather | solution.py:43
  20.3 339.9 %copy-start.1 = (bf16[1,2,14336]{2,1,0:T(2,128)(2,1)S(1)}, bf16[1,2,14336]{2,1,0:T(2,128)(2,1)}, u32[]{:S(2)}) copy-start(bf16[1,2,14336]{2,1,0:T(2,128)(2,1)} %param.5) | copy-start | bytes 172036
Sparse Core Ops, SparseCore 0:
  363.1 104.0 all-gather.1
